TPU v7x, 256 devices: a whole 4x4x8 slice. The times are simulated.
256 devices in a mesh: ia: 4 (over y), ja: 8 (over x, core), ka: 8 (over z).
Axes of the slice: x: 4, y: 4, z: 8, core: 2. Of those that a mesh axis runs over, the one named last changes fastest.
Arguments:
- observed: bfloat16 [4, 8, 40, 128, 32, 128], P('ia', 'ja', 'ka'), may hold values from -6 to 6
- weights: bfloat16 [4, 8, 40, 128, 32, 128], P('ia', 'ja', 'ka'), may hold values from 0 to 4, as said below
- coords: int32 [4, 8, 40, 3], P('ia', 'ja', 'ka'), may hold values from 0 to 31, as said below
- counts: int32 [4, 8, 8], P('ia', 'ja', 'ka'), may hold values from 0 to 5, as said below
- factor_rows: bfloat16 [64, 4096], P(None, ('ia', 'ja', 'ka')), may hold values from -0.75 to 0.75
- factor_cols: bfloat16 [64, 4096], P(None, ('ja', 'ka')), may hold values from -0.75 to 0.75
- factor_depth: bfloat16 [64, 1024], replicated, may hold values from -0.75 to 0.75
- core_tensor: bfloat16 [64, 64, 64], replicated, may hold values from -6 to 6
Outputs:
- rows_gradient: float32 [64, 4096], P(None, ('ia', 'ja', 'ka'))
- cols_gradient: float32 [64, 4096], P(None, ('ja', 'ka'))
- depth_gradient: float32 [64, 1024], P(None, 'ka')
- core_gradient: float32 [64, 64, 64], replicated
Inputs may be any that keep to these rules, and one draw needn't show every extreme that they name: counts[a, b, c] is the number of live slots of the device at index a of ia, b of ja, c of ka; the busiest devices hold 5. coords[a, b, c * 5 + s] = (p, q, t) with a * 8 <= p < (a + 1) * 8, b * 4 <= q < (b + 1) * 4, c * 4 <= t < (c + 1) * 4; the 5 slots of one device name distinct blocks. `weights`: zero at unobserved entries, positive at observed ones.
All inputs are finite; a program needn't handle non-finite values.
Results may differ from a plain program's by a relative error of at most 0.0012.
Values may be sent and summed in bfloat16 or wider, within the bound.
A program may use at most 64 MiB of HBM per device.

v0:
```python
import jax
import jax.numpy as jnp
from jax import lax
from jax.sharding import PartitionSpec as P

resid_scale = 1.0 / 64.0


def block_terms(observed_block, weight_block, row_factor, col_factor, depth_factor, core_tensor):
    rank_width, block_rows = row_factor.shape
    block_cols = col_factor.shape[1]
    slab_depth = depth_factor.shape[1]
    core_flat = core_tensor.reshape(rank_width * rank_width, rank_width)
    first_cube = jnp.dot(core_flat, depth_factor, preferred_element_type=jnp.float32).astype(
        jnp.bfloat16
    )
    first_cube = first_cube.reshape(rank_width, rank_width, slab_depth)
    second_cube = jnp.einsum(
        "rsk,sj->rkj", first_cube, col_factor, preferred_element_type=jnp.float32
    ).astype(jnp.bfloat16)
    second_flat = second_cube.reshape(rank_width, slab_depth * block_cols)
    model_block = lax.dot_general(
        row_factor, second_flat, (((0,), (0,)), ((), ())), preferred_element_type=jnp.float32
    )
    weight_flat = weight_block.reshape(block_rows, slab_depth * block_cols).astype(jnp.float32)
    data_flat = observed_block.reshape(block_rows, slab_depth * block_cols).astype(jnp.float32)
    residual = (weight_flat * (model_block - data_flat) * resid_scale).astype(jnp.bfloat16)
    row_term = lax.dot_general(
        second_flat, residual, (((1,), (1,)), ((), ())), preferred_element_type=jnp.float32
    )
    first_back = jnp.dot(row_factor, residual, preferred_element_type=jnp.float32).astype(
        jnp.bfloat16
    )
    back_cube = first_back.reshape(rank_width, slab_depth, block_cols)
    col_term = jnp.einsum("rsk,rkj->sj", first_cube, back_cube, preferred_element_type=jnp.float32)
    second_back = jnp.einsum(
        "sj,rkj->rsk", col_factor, back_cube, preferred_element_type=jnp.float32
    ).astype(jnp.bfloat16)
    back_flat = second_back.reshape(rank_width * rank_width, slab_depth)
    depth_term = lax.dot_general(
        core_flat, back_flat, (((0,), (0,)), ((), ())), preferred_element_type=jnp.float32
    )
    core_term = lax.dot_general(
        back_flat, depth_factor, (((1,), (1,)), ((), ())), preferred_element_type=jnp.float32
    )
    return (row_term, col_term, depth_term, core_term.reshape(rank_width, rank_width, rank_width))


def add_columns(table, piece, start_col):
    width = piece.shape[1]
    return lax.dynamic_update_slice_in_dim(
        table, lax.dynamic_slice_in_dim(table, start_col, width, 1) + piece, start_col, 1
    )


def accumulate_blocks(
    live_count,
    data_slots,
    weight_slots,
    coord_slots,
    row_table,
    col_table,
    factor_depth,
    core_tensor,
    row_base,
    col_base,
):
    rank_width = core_tensor.shape[0]
    block_rows = data_slots.shape[1]
    slab_depth = data_slots.shape[2]
    block_cols = data_slots.shape[3]
    start_sums = (
        jnp.zeros((rank_width, row_table.shape[1]), jnp.float32),
        jnp.zeros((rank_width, col_table.shape[1]), jnp.float32),
        jnp.zeros((rank_width, factor_depth.shape[1]), jnp.float32),
        jnp.zeros((rank_width, rank_width, rank_width), jnp.float32),
    )

    def add_slot(slot_index, running):
        rows_sum, cols_sum, depth_sum, core_sum = running
        position = coord_slots[slot_index]
        row_start = (position[0] - row_base) * block_rows
        col_start = (position[1] - col_base) * block_cols
        depth_start = position[2] * slab_depth
        row_factor = lax.dynamic_slice_in_dim(row_table, row_start, block_rows, 1)
        col_factor = lax.dynamic_slice_in_dim(col_table, col_start, block_cols, 1)
        depth_factor = lax.dynamic_slice_in_dim(factor_depth, depth_start, slab_depth, 1)
        block_sums = block_terms(
            data_slots[slot_index],
            weight_slots[slot_index],
            row_factor,
            col_factor,
            depth_factor,
            core_tensor,
        )
        rows_sum = add_columns(rows_sum, block_sums[0], row_start)
        cols_sum = add_columns(cols_sum, block_sums[1], col_start)
        depth_sum = add_columns(depth_sum, block_sums[2], depth_start)
        return (rows_sum, cols_sum, depth_sum, core_sum + block_sums[3])

    return lax.fori_loop(0, live_count, add_slot, start_sums)


def on_device(
    observed, weights, coords, counts, factor_rows, factor_cols, factor_depth, core_tensor
):
    slot_count = observed.shape[2]
    data_slots = observed.reshape(observed.shape[2:])
    weight_slots = weights.reshape(weights.shape[2:])
    coord_slots = coords.reshape(slot_count, 3)
    own_count = counts.reshape(())
    row_table = lax.all_gather(factor_rows, ("ja", "ka"), axis=1, tiled=True)
    col_table = lax.all_gather(factor_cols, "ka", axis=1, tiled=True)
    row_base = lax.axis_index("ia") * (row_table.shape[1] // observed.shape[3])
    col_base = lax.axis_index("ja") * (col_table.shape[1] // observed.shape[5])
    rows_sum, cols_sum, depth_sum, core_sum = accumulate_blocks(
        own_count,
        data_slots,
        weight_slots,
        coord_slots,
        row_table,
        col_table,
        factor_depth,
        core_tensor,
        row_base,
        col_base,
    )
    rows_gradient = lax.psum_scatter(rows_sum, ("ja", "ka"), scatter_dimension=1, tiled=True)
    cols_whole = lax.psum(cols_sum, "ia")
    depth_whole = lax.psum(depth_sum, ("ia", "ja"))
    cols_gradient, depth_gradient = (
        lax.psum_scatter(cols_whole, "ka", scatter_dimension=1, tiled=True),
        lax.psum_scatter(depth_whole, "ka", scatter_dimension=1, tiled=True),
    )
    core_gradient = lax.psum(core_sum, ("ia", "ja", "ka"))
    return (rows_gradient, cols_gradient, depth_gradient, core_gradient)


def solution(mesh):
    in_specs = (
        P("ia", "ja", "ka", None, None, None),
        P("ia", "ja", "ka", None, None, None),
        P("ia", "ja", "ka", None),
        P("ia", "ja", "ka"),
        P(None, ("ia", "ja", "ka")),
        P(None, ("ja", "ka")),
        P(),
        P(),
    )
    out_specs = (P(None, ("ia", "ja", "ka")), P(None, ("ja", "ka")), P(None, "ka"), P())
    return jax.shard_map(
        on_device, mesh=mesh, in_specs=in_specs, out_specs=out_specs, check_vma=False
    )
```

profile of v0, /device:TPU:2, one launch (start us, length us, event | category | flops | bytes accessed | tf_op | source)
XLA Modules:
  0.0 616.1 jit_solution(5447334796632463020)
XLA Ops:
  8.0 46.2 %all_gather.7 = bf16[64,1024]{0,1:T(8,128)(2,1)S(1)} all-gather(bf16[64,16]{0,1:T(8,128)(2,1)} %param.14), channel_id=1, replica_groups=mesh['ia'=4,'ja'=8,'ka'=8] {'ja','ka'}, dimensions={1}, use_global_device_ids=true | all-gather | bytes 133120 | tf_op jit(solution)/shard_map/all_gather | solution.py:112
  54.3 1.1 copy.25
  55.5 0.8 copy.23
  56.3 24.6 %all_gather.6 = bf16[64,512]{0,1:T(8,128)(2,1)S(1)} all-gather(bf16[64,64]{0,1:T(8,128)(2,1)S(1)} %copy.23), channel_id=1, replica_groups=mesh['ia'=4,'ja'=8,'ka'=8] {'ka'}, dimensions={1}, use_global_device_ids=true | all-gather | bytes 73728 | tf_op jit(solution)/shard_map/all_gather | solution.py:113
  81.0 0.7 copy.56
  81.7 1.6 broadcast_in_dim.7
  83.3 70.1 %while.16 = (s32[]{:T(128)}, f32[64,1024]{1,0:T(8,128)S(1)}, f32[64,512]{1,0:T(8,128)S(1)}, f32[64,1024]{0,1:T(8,128)S(1)}, f32[64,64,64]{2,1,0:T(8,128)}, /*ind...) while((s32[]{:T(128)}, f32[64,1024]{1,0:T(8,128)S(1)}, ...), condition=%wide.region_1.0_spmd, body=%wide.region_0.0_spmd.sunk | while | flops 356534272 | bytes 34849308 | solution.py:101
  84.1 0.6 fusion.87
  88.0 2.1 dynamic-slice_convert_fusion.3
  90.1 2.7 fusion.89
  93.5 0.9 copy-done.1
  94.4 0.7 convolution_add_fusion.3
  95.4 1.0 copy-done.2
  98.0 0.6 fusion.87
  101.9 2.1 dynamic-slice_convert_fusion.3
  104.0 2.7 fusion.89
  107.4 0.9 copy-done.1
  108.3 0.7 convolution_add_fusion.3
  109.3 1.0 copy-done.2
  111.8 0.6 fusion.87
  115.7 2.1 dynamic-slice_convert_fusion.3
  117.9 2.7 fusion.89
  121.3 0.9 copy-done.1
  122.2 0.7 convolution_add_fusion.3
  123.2 1.0 copy-done.2
  125.7 0.6 fusion.87
  129.6 2.1 dynamic-slice_convert_fusion.3
  131.8 2.7 fusion.89
  135.2 0.9 copy-done.1
  136.0 0.7 convolution_add_fusion.3
  137.1 1.0 copy-done.2
  139.6 0.6 fusion.87
  143.5 2.1 dynamic-slice_convert_fusion.3
  145.6 2.7 fusion.89
  149.0 0.9 copy-done.1
  149.9 0.7 convolution_add_fusion.3
  150.9 1.0 copy-done.2
  153.4 1.0 copy.28
  154.5 0.8 copy.31
  155.4 0.9 copy.29
  156.4 0.7 all-reduce.4.cloned.1.call-update
  158.3 179.5 %all-reduce.6.cloned.1.call-done = f32[64,1024]{0,1:T(8,128)} async-done(((f32[64,1024]{0,1:T(8,128)}), f32[64,1024]{0,1:T(8,128)}) %all-reduce.6.cloned.1.call-update) | async-done | bytes 262160
  337.8 1.3 constant_dynamic-slice_fusion.1
  339.1 0.8 copy.32
  340.0 17.6 %psum.24 = f32[64,64]{1,0:T(8,128)} all-reduce(f32[64,64]{1,0:T(8,128)S(1)} %copy.32), channel_id=1, replica_groups=mesh['ia'=4,'ja'=8,'ka'=8] {'ia'}, use_global_device_ids=true, to_apply=%region_3.0 | all-reduce | flops 4096 | bytes 32768 | tf_op jit(solution)/shard_map/psum | solution.py:129
  357.6 119.0 %psum.25 = f32[64,128]{1,0:T(8,128)} all-reduce(f32[64,128]{1,0:T(8,128)} %reduce-scatter.5.cloned.1.call-done), channel_id=1, replica_groups=mesh['ia'=4,'ja'=8,'ka'=8] {'ia','ja'}, use_global_device_ids=true, to_apply=%region_5.0 | all-reduce | flops 8192 | bytes 65536 | tf_op jit(solution)/shard_map/psum | solution.py:130
  476.6 129.0 %all-reduce.4.cloned.1.call-done = f32[64,64,64]{2,1,0:T(8,128)} async-done(((f32[64,64,64]{2,1,0:T(8,128)}), f32[64,64,64]{2,1,0:T(8,128)}) %all-reduce.4.cloned.1.call-update) | async-done | bytes 1048592 | tf_op jit(solution)/shard_map/psum | solution.py:135
  605.5 3.2 copy.91
  (79 shorter events, 17.5 us)
Async XLA Ops:
  8.0 329.8 %all-reduce.6.cloned.1.call-start = ((), (), s32[]{:S(2)}) async-start(), calls=%async_computation.5 | async-start | bytes 1048576
  54.2 29.1 %copy-start = (bf16[64,64,64]{2,1,0:T(8,128)(2,1)S(1)}, bf16[64,64,64]{2,1,0:T(8,128)(2,1)}, u32[]{:S(2)}) copy-start(bf16[64,64,64]{2,1,0:T(8,128)(2,1)} %param.17) | copy-start | bytes 1572868
  92.8 1.6 copy-start.1
  95.1 1.3 copy-start.2
  106.7 1.6 copy-start.1
  109.0 1.3 copy-start.2
  120.6 1.6 copy-start.1
  122.8 1.3 copy-start.2
  134.4 1.6 copy-start.1
  136.7 1.3 copy-start.2
  148.3 1.6 copy-start.1
  150.6 1.3 copy-start.2
  154.4 2.7 copy-start.3
  154.4 184.7 %reduce-scatter.7.cloned.1.call-start = ((), (), s32[]{:S(2)}) async-start(), calls=%async_computation.4 | async-start | bytes 294912
  155.3 202.3 %reduce-scatter.5.cloned.1.call-start = ((), (), s32[]{:S(2)}) async-start(), calls=%async_computation.3 | async-start | bytes 294912 | tf_op jit(solution)/shard_map/reduce_scatter | solution.py:133
  156.3 449.2 %all-reduce.4.cloned.1.call-start = ((), (), s32[]{:S(2)}) async-start(), calls=%async_computation.2 | async-start | bytes 4194304 | tf_op jit(solution)/shard_map/psum | solution.py:135
Sparse Core Ops, SparseCore 0:
  154.6 183.2 all-reduce.5
  343.8 261.6 all-reduce.3
Sparse Core Ops, SparseCore 1:
  157.4 36.2 reduce-scatter.6
  196.0 35.9 reduce-scatter.4
where the time goes:
time: 617 us; the launch traced here: 616 us
  waiting for transfers between devices  309 us (50%)
  blocking collectives  207 us (34%)
  matrix products  29.4 us (5%)
  local copies, waits for them, and re-layouts  29.1 us (5%)
  between operations  16.2 us (3%)
  loops' own time  14 us (2%)
  other arithmetic  10.7 us (2%)
    unnamed x6, waiting for transfers between devices  180 us
    psum x1, waiting for transfers between devices, on_device(): core_gradient = lax.psum(core_sum, ('ia', 'ja', 'ka'))  129 us
    psum x1, blocking collectives, on_device(): depth_whole = lax.psum(depth_sum, ('ia', 'ja'))  119 us
    all_gather x1, blocking collectives, on_device(): row_table = lax.all_gather(factor_rows, ('ja', 'ka'), axis=1, tiled=True)  46.2 us
    all_gather x1, blocking collectives, on_device(): col_table = lax.all_gather(factor_cols, 'ka', axis=1, tiled=True)  24.6 us
    psum x1, blocking collectives, on_device(): cols_whole = lax.psum(cols_sum, 'ia')  17.6 us
    another operation x1, loops' own time, accumulate_blocks(): return lax.fori_loop(0, live_count, add_slot, start_sums)  14 us
    dot_general x5, matrix products, block_terms(): lax.dot_general(row_factor, second_flat, (((0,), (0,)), ((), ())), prefer...  13.4 us
  transfers between devices with their start and end apart: 4, of which 2 were waited for; matrix products, arithmetic and copies ran while one was open for 1% of the time, Pallas kernels for 0%

commit v1 on v0

--- a/solution.py
+++ b/solution.py
@@ -132,7 +132,7 @@
         lax.psum_scatter(cols_whole, "ka", scatter_dimension=1, tiled=True),
         lax.psum_scatter(depth_whole, "ka", scatter_dimension=1, tiled=True),
     )
-    core_gradient = lax.psum(core_sum, ("ia", "ja", "ka"))
+    core_gradient = lax.psum(lax.psum(core_sum, ("ja", "ka")), "ia")
     return (rows_gradient, cols_gradient, depth_gradient, core_gradient)
 
 

time: 617 us -> 502 us (0.81)
  waiting for transfers between devices: 309 us -> 190 us
    psum x1, waiting for transfers between devices: 129 us -> 0.01 us  [on_device(): core_gradient = lax.psum(lax.psum(core_sum, ('ja', 'ka')), 'ia')]
    unnamed x6, waiting for transfers between devices: 180 us -> 190 us
  transfers between devices with their start and end apart: 4 -> 4, of which waited for: 2 -> 1; matrix products, arithmetic and copies ran while one was open for 1% -> 1% of each run, Pallas kernels for 0% -> 0%
where the time goes in v1:
time: 502 us; the launch traced here: 498 us
  blocking collectives  209 us (42%)
  waiting for transfers between devices  190 us (38%)
  matrix products  29.4 us (6%)
  local copies, waits for them, and re-layouts  28.9 us (6%)
  between operations  16.2 us (3%)
  loops' own time  13.6 us (3%)
  other arithmetic  10.7 us (2%)
    unnamed x6, waiting for transfers between devices  190 us
    psum x1, blocking collectives, on_device(): depth_whole = lax.psum(depth_sum, ('ia', 'ja'))  120 us
    all_gather x1, blocking collectives, on_device(): row_table = lax.all_gather(factor_rows, ('ja', 'ka'), axis=1, tiled=True)  46.2 us
    all_gather x1, blocking collectives, on_device(): col_table = lax.all_gather(factor_cols, 'ka', axis=1, tiled=True)  24.6 us
    psum x1, blocking collectives, on_device(): cols_whole = lax.psum(cols_sum, 'ia')  18.1 us
    another operation x1, loops' own time, accumulate_blocks(): return lax.fori_loop(0, live_count, add_slot, start_sums)  13.6 us
    dot_general x5, matrix products, block_terms(): lax.dot_general(row_factor, second_flat, (((0,), (0,)), ((), ())), prefer...  13.3 us
    convert_element_type x5, other arithmetic, block_terms(): observed_block.reshape(block_rows, slab_depth * block_cols)  10.7 us
  transfers between devices with their start and end apart: 4, of which 1 were waited for; matrix products, arithmetic and copies ran while one was open for 1% of the time, Pallas kernels for 0%

profile of v1, /device:TPU:2, one launch (start us, length us, event | category | flops | bytes accessed | tf_op | source)
XLA Modules:
  0.0 497.6 jit_solution(12647583901594769200)
XLA Ops:
  8.0 46.2 %all_gather.7 = bf16[64,1024]{0,1:T(8,128)(2,1)S(1)} all-gather(bf16[64,16]{0,1:T(8,128)(2,1)} %param.14), channel_id=1, replica_groups=mesh['ia'=4,'ja'=8,'ka'=8] {'ja','ka'}, dimensions={1}, use_global_device_ids=true | all-gather | bytes 133120 | tf_op jit(solution)/shard_map/all_gather | solution.py:112
  54.3 1.1 copy.25
  55.5 0.8 copy.23
  56.3 24.6 %all_gather.6 = bf16[64,512]{0,1:T(8,128)(2,1)S(1)} all-gather(bf16[64,64]{0,1:T(8,128)(2,1)S(1)} %copy.23), channel_id=1, replica_groups=mesh['ia'=4,'ja'=8,'ka'=8] {'ka'}, dimensions={1}, use_global_device_ids=true | all-gather | bytes 73728 | tf_op jit(solution)/shard_map/all_gather | solution.py:113
  81.0 0.7 copy.56
  81.7 1.6 broadcast_in_dim.7
  83.3 69.4 %while.16 = (s32[]{:T(128)}, f32[64,1024]{1,0:T(8,128)S(1)}, f32[64,512]{1,0:T(8,128)S(1)}, f32[64,1024]{0,1:T(8,128)S(1)}, f32[64,64,64]{2,1,0:T(8,128)}, /*ind...) while((s32[]{:T(128)}, f32[64,1024]{1,0:T(8,128)S(1)}, ...), condition=%wide.region_1.0_spmd, body=%wide.region_0.0_spmd.sunk | while | flops 356534272 | bytes 34849308 | solution.py:101
  84.1 0.6 fusion.87
  85.6 0.6 reshape.62
  87.9 2.1 dynamic-slice_convert_fusion.3
  90.0 2.7 fusion.89
  93.4 0.9 copy-done.1
  94.3 0.7 convolution_add_fusion.3
  95.3 1.0 copy-done.2
  99.4 0.6 reshape.62
  101.6 2.1 dynamic-slice_convert_fusion.3
  103.8 2.7 fusion.89
  107.1 0.9 copy-done.1
  108.0 0.7 convolution_add_fusion.3
  109.0 1.0 copy-done.2
  113.1 0.6 reshape.62
  115.4 2.1 dynamic-slice_convert_fusion.3
  117.5 2.7 fusion.89
  120.9 0.9 copy-done.1
  121.8 0.7 convolution_add_fusion.3
  122.8 1.0 copy-done.2
  126.9 0.6 reshape.62
  129.1 2.1 dynamic-slice_convert_fusion.3
  131.2 2.7 fusion.89
  134.6 0.9 copy-done.1
  135.5 0.7 convolution_add_fusion.3
  136.5 1.0 copy-done.2
  140.6 0.6 reshape.62
  142.9 2.1 dynamic-slice_convert_fusion.3
  145.0 2.7 fusion.89
  148.4 0.9 copy-done.1
  149.3 0.7 convolution_add_fusion.3
  150.3 1.0 copy-done.2
  152.7 1.0 copy.28
  153.8 0.8 copy.31
  154.7 0.9 copy.29
  155.7 189.9 %all-reduce.7.cloned.1.call-done = (f32[64,1024]{0,1:T(8,128)}, f32[64,64,64]{2,1,0:T(8,128)}) async-done(((f32[64,1024]{0,1:T(8,128)}, f32[64,64,64]{2,1,0:T(8,128)}), (f32[64,1024]{0,1:T(8,128)}, f32[64,64,64]{2,1,0:T(8,128)})) %all-reduce.7.cloned.1.call-update) | async-done | bytes 1310736
  345.6 0.6 dynamic-slice
  346.9 0.8 copy.32
  347.7 18.1 %psum.32 = f32[64,64]{1,0:T(8,128)} all-reduce(f32[64,64]{1,0:T(8,128)S(1)} %copy.32), channel_id=1, replica_groups=mesh['ia'=4,'ja'=8,'ka'=8] {'ia'}, use_global_device_ids=true, to_apply=%region_3.0 | all-reduce | flops 4096 | bytes 32768 | tf_op jit(solution)/shard_map/psum | solution.py:129
  365.9 119.9 %psum.33 = f32[64,128]{1,0:T(8,128)} all-reduce(f32[64,128]{1,0:T(8,128)} %reduce-scatter.5.cloned.1.call-done), channel_id=1, replica_groups=mesh['ia'=4,'ja'=8,'ka'=8] {'ia','ja'}, use_global_device_ids=true, to_apply=%region_5.0 | all-reduce | flops 8192 | bytes 65536 | tf_op jit(solution)/shard_map/psum | solution.py:130
  485.7 1.3 constant_dynamic-slice_fusion.1
  487.0 3.2 copy.92
  (79 shorter events, 16.4 us)
Async XLA Ops:
  8.0 337.6 %all-reduce.7.cloned.1.call-start = ((), (), s32[]{:S(2)}) async-start(), calls=%async_computation.5 | async-start | bytes 5242880
  54.2 29.1 %copy-start = (bf16[64,64,64]{2,1,0:T(8,128)(2,1)S(1)}, bf16[64,64,64]{2,1,0:T(8,128)(2,1)}, u32[]{:S(2)}) copy-start(bf16[64,64,64]{2,1,0:T(8,128)(2,1)} %param.17) | copy-start | bytes 1572868
  92.7 1.6 copy-start.1
  94.9 1.3 copy-start.2
  106.4 1.6 copy-start.1
  108.7 1.3 copy-start.2
  120.2 1.6 copy-start.1
  122.4 1.3 copy-start.2
  133.9 1.6 copy-start.1
  136.2 1.3 copy-start.2
  147.7 1.6 copy-start.1
  149.9 1.3 copy-start.2
  153.8 191.9 %copy-start.3 = (u32[256]{0:T(256)S(1)}, u32[256]{0:T(256)}, u32[]{:S(2)}) copy-start(u32[256]{0:T(256)} %constant.44) | copy-start | bytes 3076
  153.8 193.1 %reduce-scatter.7.cloned.1.call-start = ((), (), s32[]{:S(2)}) async-start(), calls=%async_computation.4 | async-start | bytes 294912
  154.7 211.2 %reduce-scatter.5.cloned.1.call-start = ((), (), s32[]{:S(2)}) async-start(), calls=%async_computation.3 | async-start | bytes 294912 | tf_op jit(solution)/shard_map/reduce_scatter | solution.py:133
  155.7 331.4 %all-reduce.5.cloned.1.call-start = ((), (), s32[]{:S(2)}) async-start(), calls=%async_computation.2 | async-start | bytes 4194304 | tf_op jit(solution)/shard_map/psum | solution.py:135
Sparse Core Ops, SparseCore 0:
  153.9 191.6 all-reduce.6
  347.9 62.9 all-reduce.4
Sparse Core Ops, SparseCore 1:
  156.7 36.1 reduce-scatter.6
  195.3 36.0 reduce-scatter.4
